TPU v7x, 32 devices: a whole 2x2x4 slice. The times are simulated.
32 devices in a mesh: fsdp: 16 (over z, y, core), frame: 2 (over x).
Axes of the slice: x: 2, y: 2, z: 4, core: 2. Of those that a mesh axis runs over, the one named last changes fastest.
Arguments:
- student_tokens: bfloat16 [16, 8, 256, 3200], P('fsdp', 'frame'), may hold values from -6 to 6
- norm_gain: float32 [3200], replicated, may hold values from 0.1 to 1.9
- mae_weight: bfloat16 [3200, 1408], P('fsdp'), may hold values from -0.109375 to 0.109375
- clip_target: bfloat16 [16, 8, 3200], P('fsdp', 'frame'), may hold values from -6 to 6
- mae_target: bfloat16 [16, 8, 128, 1408], P('fsdp', 'frame'), may hold values from -6 to 6
- keep_mask: int32 [16, 8, 256], P('fsdp', 'frame'), may hold values 0 or 1
- teacher_gate: int32 [16], P('fsdp'), may hold values from 0 to 2
- temp_bucket: int32 [16], P('fsdp'), may hold values from 0 to 3
Outputs:
- token_grad: bfloat16 [16, 8, 256, 3200], P('fsdp', 'frame')
- weight_grad: float32 [3200, 1408], P('fsdp')
- gain_grad: float32 [3200], replicated
- loss: float32 [], replicated
Inputs may be any that keep to these rules, and one draw needn't show every extreme that they name: `teacher_gate`: 0 aligns a clip to both teachers, 1 to InternVL only, 2 to VideoMAE-g only.
All inputs are finite; a program needn't handle non-finite values. No bound on the sum of `keep_mask` on one device may be relied on, other than what follows from the above.
Results may differ from a plain program's by a relative error of at most 0.011.
Values may be sent and summed in bfloat16 or wider, within the bound.
A program may use at most 128 MiB of HBM per device.

v0:
```python
import jax
import jax.numpy as jnp
from jax import lax
from jax.sharding import PartitionSpec as P

epsilon = 1e-06


def swapped(shard, axis, stride):
    return lax.ppermute(shard, axis, [(i, i ^ 1 << stride) for i in range(lax.axis_size(axis))])


def unit_rows(values):
    inverse = lax.rsqrt(jnp.mean(values * values, axis=-1, keepdims=True) + epsilon)
    return (values * inverse, inverse)


def unit_grad(errors, unit, inverse):
    return inverse * (errors - unit * jnp.mean(errors * unit, axis=-1, keepdims=True))


def over_rows(left, right):
    return lax.dot_general(
        left, right, (((0,), (0,)), ((), ())), preferred_element_type=jnp.float32
    )


def back_project(grads, weight):
    return (
        0.5
        * lax.dot_general(
            grads, weight, (((1,), (1,)), ((), ())), preferred_element_type=jnp.float32
        )
    ).astype(jnp.bfloat16)


def per_device(
    student_tokens,
    norm_gain,
    mae_weight,
    clip_target,
    mae_target,
    keep_mask,
    teacher_gate,
    temp_bucket,
):
    samples, frames_here, patches, model_width = student_tokens.shape
    half_rows = patches // 2
    channels = mae_weight.shape[1]
    frame_devices = lax.axis_size("frame")
    top_bit = frame_devices.bit_length() - 2
    weight = lax.all_gather(mae_weight, "fsdp", axis=0, tiled=True)
    token_float = student_tokens.astype(jnp.float32)
    recip = lax.rsqrt(jnp.mean(token_float * token_float, axis=-1, keepdims=True) + epsilon)
    normed = (token_float * recip * norm_gain).astype(jnp.bfloat16)
    keep_float = keep_mask.astype(jnp.float32)
    pooled = (
        jnp.einsum(
            "bfp,bfpd->bfd",
            keep_mask.astype(jnp.bfloat16),
            normed,
            preferred_element_type=jnp.float32,
        )
        / patches
    )
    clip_unit, clip_inverse = unit_rows(pooled)
    teach_unit, unused_one = unit_rows(clip_target.astype(jnp.float32))
    clip_err = clip_unit - teach_unit
    clip_loss = 0.5 * jnp.sum(clip_err * clip_err, axis=-1)
    scaling = jnp.exp2(temp_bucket.astype(jnp.float32))
    clip_on = (teacher_gate != 2).astype(jnp.float32)
    mae_on = (teacher_gate != 1).astype(jnp.float32)
    parity = lax.axis_index("frame") // (frame_devices // 2)
    halves = normed.reshape(samples, frames_here, 2, half_rows, model_width)
    mask_halves = keep_mask.astype(jnp.bfloat16).reshape(samples, frames_here, 2, half_rows)
    own_half = lax.dynamic_slice_in_dim(halves, parity, 1, 2)[:, :, 0]
    sent_half = lax.dynamic_slice_in_dim(halves, 1 - parity, 1, 2)[:, :, 0]
    own_mask = lax.dynamic_slice_in_dim(mask_halves, parity, 1, 2)[:, :, 0]
    sent_mask = lax.dynamic_slice_in_dim(mask_halves, 1 - parity, 1, 2)[:, :, 0]
    got_half, got_mask = swapped((sent_half, sent_mask), "frame", top_bit)
    first_rows = own_half.reshape(-1, model_width)
    second_rows = got_half.reshape(-1, model_width)
    live = (own_mask.astype(jnp.float32) * got_mask.astype(jnp.float32)).reshape(samples, -1)
    projected = 0.5 * (
        jnp.dot(first_rows, weight, preferred_element_type=jnp.float32)
        + jnp.dot(second_rows, weight, preferred_element_type=jnp.float32)
    )
    proj_unit, proj_inverse = unit_rows(projected)
    target_unit, unused_two = unit_rows(mae_target.reshape(-1, channels).astype(jnp.float32))
    mae_err = proj_unit - target_unit
    mae_loss = (0.5 * jnp.sum(mae_err * mae_err, axis=-1)).reshape(samples, -1)
    sample_loss = scaling * (
        clip_on * jnp.sum(clip_loss, axis=1) + mae_on * jnp.sum(live * mae_loss, axis=1)
    )
    row_scale = ((scaling * mae_on)[:, None] * live).reshape(-1)
    row_grad = (row_scale[:, None] * unit_grad(mae_err, proj_unit, proj_inverse)).astype(
        jnp.bfloat16
    )
    shard = lax.psum_scatter(
        0.5 * (over_rows(first_rows, row_grad) + over_rows(second_rows, row_grad)),
        "fsdp",
        scatter_dimension=0,
        tiled=True,
    )
    shard = lax.psum_scatter(shard, "frame", scatter_dimension=1, tiled=True)
    shard = lax.all_gather(shard, "frame", axis=1, tiled=True)
    clip_count = samples * lax.axis_size("fsdp")
    weight_grad = shard / clip_count
    pair_grad = back_project(row_grad, weight).reshape(samples, frames_here, half_rows, model_width)
    returned = swapped(pair_grad, "frame", top_bit)
    lower_first = jnp.stack([pair_grad, returned], axis=2)
    upper_first = jnp.stack([returned, pair_grad], axis=2)
    spread = jnp.where(parity == 0, lower_first, upper_first)
    spread = spread.reshape(samples, frames_here, patches, model_width).astype(jnp.float32)
    clip_grad = (scaling * clip_on)[:, None, None] * unit_grad(clip_err, clip_unit, clip_inverse)
    normed_grad = spread + keep_float[:, :, :, None] * clip_grad[:, :, None, :] / patches
    inner = jnp.mean(normed_grad * norm_gain * token_float, axis=-1, keepdims=True)
    token_grad = (recip * (norm_gain * normed_grad - token_float * recip * recip * inner)).astype(
        jnp.bfloat16
    )
    gain_local = jnp.sum(normed_grad * token_float * recip, axis=(0, 1, 2))
    loss_local = jnp.sum(sample_loss)
    gain_total, loss_total = lax.psum((gain_local, loss_local), ("fsdp", "frame"))
    frame_count = frames_here * frame_devices
    gain_grad = gain_total / clip_count
    loss = loss_total / (clip_count * frame_count * patches * channels)
    return (token_grad, weight_grad, gain_grad, loss)


def solution(mesh):
    placed = (
        P("fsdp", "frame", None, None),
        P(),
        P("fsdp", None),
        P("fsdp", "frame", None),
        P("fsdp", "frame", None, None),
        P("fsdp", "frame", None),
        P("fsdp"),
        P("fsdp"),
    )
    return jax.shard_map(
        per_device,
        mesh=mesh,
        in_specs=placed,
        out_specs=(P("fsdp", "frame", None, None), P("fsdp", None), P(), P()),
        check_vma=False,
    )
```

profile of v0, /device:TPU:0, one launch (start us, length us, event | category | flops | bytes accessed | tf_op | source)
XLA Modules:
  0.0 434.5 jit_solution(7674785082313607338)
XLA Ops:
  8.0 4.4 %fusion.7 = f32[4,256]{1,0:T(4,128)S(1)} fusion(bf16[1,4,256,3200]{3,2,1,0:T(8,128)(2,1)} %param.8), kind=kLoop, calls=%fused_computation.12 | loop fusion | flops 9829376 | bytes 6557696 | tf_op jit(solution)/shard_map/reduce_sum | solution.py:54
  12.7 2.6 fusion.2
  15.3 3.2 dynamic-slice_bitcast_fusion
  18.6 1.7 copy-done.1
  20.2 3.2 collective-permute-start.1
  25.3 65.8 %all-gather.4.cloned.1.call-done = bf16[3200,1408]{1,0:T(8,128)(2,1)} async-done(((bf16[200,1408]{1,0:T(8,128)(2,1)}), bf16[3200,1408]{1,0:T(8,128)(2,1)}) %all-gather.4.cloned.1.call-update) | async-done | bytes 9011216 | tf_op jit(solution)/shard_map/all_gather | solution.py:52
  91.1 9.5 %fusion.26 = f32[512,1408]{1,0:T(8,128)S(1)} fusion(bf16[512,3200]{1,0:T(8,128)(2,1)} %bitcast.116, bf16[3200,1408]{1,0:T(8,128)(2,1)} %all-gather.4.cloned.1.call-done), kind=kOutput, calls=%fused_computation.71 | convolution fusion | flops 4613734400 | bytes 15171584 | tf_op jit(solution)/shard_map/dot_general | solution.py:85
  100.7 7.5 %multiply_reduce_fusion.3 = (f32[512]{0:T(512)S(1)}, f32[512,1408]{1,0:T(8,128)S(1)}) fusion(f32[512,1408]{1,0:T(8,128)S(1)} %fusion.26, bf16[512,3200]{1,0:T(8,128)(2,1)} %bitcast.8, bf16[3200,1408]{1,0:T(8,128)(2,1)S(1)} %copy-done.7), kind=kOutput, calls=%fused_computation.31 | convolution fusion | flops 4616617472 | bytes 18057216 | tf_op jit(solution)/shard_map/dot_general | solution.py:86
  110.8 9.1 %fusion.27 = f32[3200,1408]{1,0:T(8,128)} fusion(bf16[512,3200]{1,0:T(8,128)(2,1)S(1)} %bitcast.117, bf16[512,1408]{1,0:T(8,128)(2,1)S(1)} %multiply_convert_fusion), kind=kOutput, calls=%fused_computation.72 | convolution fusion | flops 4613734400 | bytes 22740992 | tf_op jit(solution)/shard_map/dot_general | solution.py:23
  119.9 13.7 %add_multiply_fusion = f32[3200,1408]{1,0:T(8,128)} fusion(f32[3200,1408]{1,0:T(8,128)} %fusion.27, bf16[512,3200]{1,0:T(8,128)(2,1)} %bitcast.8, bf16[512,1408]{1,0:T(8,128)(2,1)S(1)} %multiply_convert_fusion), kind=kOutput, calls=%fused_computation.4 | convolution fusion | flops 4622745600 | bytes 40763392 | tf_op jit(solution)/shard_map/dot_general | solution.py:23
  133.7 10.6 %fusion.14 = bf16[512,3200]{1,0:T(8,128)(2,1)} fusion(bf16[512,1408]{1,0:T(8,128)(2,1)S(1)} %multiply_convert_fusion, bf16[3200,1408]{1,0:T(8,128)(2,1)} %all-gather.4.cloned.1.call-done), kind=kOutput, calls=%fused_computation.22 | convolution fusion | flops 4617011200 | bytes 13729792 | tf_op jit(solution)/shard_map/dot_general | solution.py:31
  144.3 1.5 collective-permute-start.2
  145.9 5.0 %fusion.12 = f32[4,1,3200]{2,1,0:T(1,128)S(1)} fusion(bf16[1,4,256,3200]{3,2,1,0:T(8,128)(2,1)} %copy-done.1, bf16[4,256,1]{1,0,2:T(4,128)(2,1)S(1)} %get-tuple-element.15), kind=kOutput, calls=%fused_computation.20 | convolution fusion | flops 6553600 | bytes 6606848 | tf_op jit(solution)/shard_map/bfp,bfpd->bfd/dot_general | solution.py:58
  153.3 170.9 %reduce-scatter.9.cloned.1.call-done = f32[200,1408]{1,0:T(8,128)} async-done(((f32[3200,1408]{1,0:T(8,128)}), f32[200,1408]{1,0:T(8,128)}) %reduce-scatter.9.cloned.1.call-update) | async-done | bytes 1126416
  324.2 2.8 copy.19
  327.1 8.7 %fusion.11 = f32[1,4,2,128,3200]{4,3,1,2,0:T(8,128)} fusion(bf16[1,4,1,128,3200]{4,3,1,2,0:T(8,128)(2,1)S(1)} %bitcast.118, bf16[1,4,1,128,3200]{4,3,1,2,0:T(8,128)(2,1)} %bitcast.11, pred[]{:T(512)S(6)} %eq.3), kind=kLoop, calls=%fused_computation.19 | loop fusion | flops 13107200 | bytes 19660800 | tf_op jit(solution)/shard_map/convert_element_type | solution.py:114
  335.8 10.4 %copy.15 = f32[1,4,2,128,3200]{4,3,2,1,0:T(8,128)} copy(f32[1,4,2,128,3200]{4,3,1,2,0:T(8,128)} %fusion.11) | data formatting | bytes 26214400 | tf_op jit(solution)/shard_map/convert_element_type | solution.py:114
  346.2 9.5 %fusion.10 = (f32[3200]{0:T(1024)S(1)}, f32[4,256]{1,0:T(4,128)S(1)}) fusion(bf16[1,4,256,3200]{3,2,1,0:T(8,128)(2,1)} %param.8, f32[1,4,2,128,3200]{4,3,2,1,0:T(8,128)} %copy.15, f32[4,3200]{1,0:T(4,128)S(1)} %fusion.20, f32[4,256]{1,0:T(4,128)S(1)} %get-tuple-element.14, f32[4,256]{1,0:T(4,128)S(1)} %add_rsqrt_fusion, f32[3200]{0:T(1024)S(1)} %copy-done.5), kind=kLoop, calls=%fused_computation.15 | loop fusion | flops 32763776 | bytes 19749888 | tf_op jit(solution)/shard_map/reduce_sum | solution.py:121
  355.7 40.4 %all-reduce.1 = (f32[3200]{0:T(1024)S(1)}, f32[]{:T(128)}) all-reduce(f32[3200]{0:T(1024)S(1)} %get-tuple-element.4, f32[]{:T(128)} %bitcast.30), channel_id=1, replica_groups=mesh['fsdp'=16,'frame'=2] {'fsdp','frame'}, use_global_device_ids=true, to_apply=%region_11.12 | all-reduce | flops 3201 | bytes 25608 | tf_op jit(solution)/shard_map/psum | solution.py:123
  397.3 2.2 copy.20
  399.5 12.0 %fusion.6 = bf16[1,4,256,3200]{3,2,1,0:T(8,128)(2,1)} fusion(bf16[1,4,256,3200]{3,2,1,0:T(8,128)(2,1)} %param.8, f32[1,4,2,128,3200]{4,3,2,1,0:T(8,128)} %copy.15, f32[4,256]{1,0:T(4,128)S(1)} %broadcast_multiply_fusion.2, f32[4,3200]{1,0:T(4,128)S(1)} %fusion.20, f32[4,256]{1,0:T(4,128)S(1)} %get-tuple-element.14, f32[3200]{0:T(1024)S(1)} %copy-done.5, ...), kind=kLoop, calls=%fused_computation.11 | loop fusion | flops 36044800 | bytes 26290688 | tf_op jit(solution)/shard_map/convert_element_type | solution.py:118
  411.6 11.2 %all-gather.6.cloned.1.call-done = f32[2,704,200]{1,2,0:T(8,128)} async-done(((f32[1,704,200]{1,2,0:T(8,128)}), f32[2,704,200]{1,2,0:T(8,128)}) %all-gather.6.cloned.1.call-update) | async-done | bytes 1126416 | tf_op jit(solution)/shard_map/all_gather | solution.py:106
  422.8 1.4 broadcast_multiply_fusion
  424.8 2.0 reshape.268
  (49 shorter events, 6.9 us)
Async XLA Ops:
  7.2 5.2 %copy-start.5 = (f32[3200]{0:T(1024)S(1)}, f32[3200]{0:T(1024)}, u32[]{:S(2)}) copy-start(f32[3200]{0:T(1024)} %param.9) | copy-start | bytes 38404
  7.2 83.9 %all-gather.4.cloned.1.call-start = ((), (), s32[]{:S(2)}) async-start(), calls=%async_computation.2 | async-start | bytes 9574400 | tf_op jit(solution)/shard_map/all_gather | solution.py:52
  7.9 316.3 %reduce-scatter.9.cloned.1.call-start = ((), (), s32[]{:S(2)}) async-start(), calls=%async_computation.5 | async-start | bytes 19148800
  8.0 4.7 %copy-start = (bf16[1,4,256,3200]{3,2,1,0:T(8,128)(2,1)S(1)}, bf16[1,4,256,3200]{3,2,1,0:T(8,128)(2,1)}, u32[]{:S(2)}) copy-start(bf16[1,4,256,3200]{3,2,1,0:T(8,128)(2,1)} %param.8) | copy-start | bytes 19660804
  15.3 4.9 %copy-start.1 = (bf16[1,4,256,3200]{3,2,1,0:T(8,128)(2,1)}, bf16[1,4,256,3200]{3,2,1,0:T(8,128)(2,1)S(1)}, u32[]{:S(2)}) copy-start(bf16[1,4,256,3200]{3,2,1,0:T(8,128)(2,1)S(1)} %fusion.2) | copy-start | bytes 19660804
  15.3 8.2 %copy-start.6 = (s32[1,4,256]{2,1,0:T(4,128)S(1)}, s32[1,4,256]{2,1,0:T(4,128)}, u32[]{:S(2)}) copy-start(s32[1,4,256]{2,1,0:T(4,128)} %param.13) | copy-start | bytes 12292
  15.3 9.6 %copy-start.2 = (bf16[1,4,128,1408]{3,2,1,0:T(8,128)(2,1)S(1)}, bf16[1,4,128,1408]{3,2,1,0:T(8,128)(2,1)}, u32[]{:S(2)}) copy-start(bf16[1,4,128,1408]{3,2,1,0:T(8,128)(2,1)} %param.12) | copy-start | bytes 4325380
  20.2 80.4 %collective-permute-start.1 = (bf16[1,4,128,3200]{3,2,1,0:T(8,128)(2,1)}, bf16[1,4,128,3200]{3,2,1,0:T(8,128)(2,1)}, u32[]{:S(2)}, u32[]{:S(2)}) collective-permute-start(bf16[1,4,128,3200]{3,2,1,0:T(8,128)(2,1)} %get-tuple-element.12), channel_id=1, source_target_pairs={{0,1},{1,0},{2,3},{3,2},{4,5},{5,4},{6,7},{7,6},{8,9},{9,8},{10,11... | collective-permute-start | bytes 9830408 | tf_op jit(solution)/shard_map/ppermute | solution.py:10
  23.5 85.8 %collective-permute-start = (bf16[1,4,128]{2,1,0:T(4,128)(2,1)S(1)}, bf16[1,4,128]{2,1,0:T(4,128)(2,1)S(1)}, u32[]{:S(2)}, u32[]{:S(2)}) collective-permute-start(bf16[1,4,128]{2,1,0:T(4,128)(2,1)S(1)} %dynamic-slice_bitcast_fusion.1), channel_id=1, source_target_pairs={{0,1},{1,0},{2,3},{3,2},{4,5},{5,4},{6,7},{7,6},{8,9},{9,8},{10,11... | collective-permute-start | bytes 3080 | tf_op jit(solution)/shard_map/ppermute | solution.py:10
  91.1 9.6 %copy-start.7 = (bf16[3200,1408]{1,0:T(8,128)(2,1)S(1)}, bf16[3200,1408]{1,0:T(8,128)(2,1)}, u32[]{:S(2)}) copy-start(bf16[3200,1408]{1,0:T(8,128)(2,1)} %all-gather.4.cloned.1.call-done) | copy-start | bytes 27033604
  108.2 2.6 copy-start.3
  133.6 12.1 %copy-start.4 = (bf16[1,4,3200]{2,1,0:T(4,128)(2,1)S(1)}, bf16[1,4,3200]{2,1,0:T(4,128)(2,1)}, u32[]{:S(2)}) copy-start(bf16[1,4,3200]{2,1,0:T(4,128)(2,1)} %param.11) | copy-start | bytes 76804
  133.7 263.7 %reduce-scatter.7.cloned.1.call-start = ((), (), s32[]{:S(2)}) async-start(), calls=%async_computation.4 | async-start | bytes 2162688
  144.3 182.8 %collective-permute-start.2 = (bf16[1,4,128,3200]{3,2,1,0:T(8,128)(2,1)}, bf16[1,4,128,3200]{3,2,1,0:T(8,128)(2,1)S(1)}, u32[]{:S(2)}, u32[]{:S(2)}) collective-permute-start(bf16[1,4,128,3200]{3,2,1,0:T(8,128)(2,1)} %bitcast.12), channel_id=1, source_target_pairs={{0,1},{1,0},{2,3},{3,2},{4,5},{5,4},{6,7},{7,6},{8,9},{9,8},{10,11... | collective-permute-start | bytes 9830408 | tf_op jit(solution)/shard_map/ppermute | solution.py:10
  327.0 95.8 %all-gather.6.cloned.1.call-start = ((), (), s32[]{:S(2)}) async-start(), calls=%async_computation.3 | async-start | bytes 1843200 | tf_op jit(solution)/shard_map/all_gather | solution.py:106
Sparse Core Ops, SparseCore 0:
  10.1 80.9 all-gather.3
  133.8 190.4 reduce-scatter.8
  327.2 23.7 reduce-scatter.6
  399.7 23.0 all-gather.5
where the time goes:
time: 435 us; the launch traced here: 434 us
  waiting for transfers between devices  249 us (57%)
  matrix products  55.4 us (13%)
  other arithmetic  43.4 us (10%)
  blocking collectives  40.4 us (9%)
  local copies, waits for them, and re-layouts  23.3 us (5%)
  between operations  18.4 us (4%)
  starting transfers between devices  4.93 us (1%)
    unnamed x6, waiting for transfers between devices  172 us
    all_gather x1, waiting for transfers between devices, per_device(): weight = lax.all_gather(mae_weight, 'fsdp', axis=0, tiled=True)  65.8 us
    psum x1, blocking collectives, per_device(): lax.psum((gain_local, loss_local), ('fsdp', 'frame'))  40.4 us
    dot_general x2, matrix products, over_rows(): lax.dot_general(left, right, (((0,), (0,)), ((), ())), preferred_element_...  22.8 us
    convert_element_type x1, other arithmetic, per_device(): (recip * (norm_gain * normed_grad - token_float * recip * recip * inner))...  12 us
    all_gather x1, waiting for transfers between devices, per_device(): shard = lax.all_gather(shard, 'frame', axis=1, tiled=True)  11.2 us
    dot_general x1, matrix products, back_project(): lax.dot_general(grads, weight, (((1,), (1,)), ((), ())), preferred_elemen...  10.6 us
    convert_element_type x1, local copies, waits for them, and re-layouts, per_device(): spread.reshape(samples, frames_here, patches, model_width)  10.4 us
  transfers between devices with their start and end apart: 7, of which 3 were waited for; matrix products, arithmetic and copies ran while one was open for 21% of the time, Pallas kernels for 0%

commit v1 on v0

--- a/solution.py
+++ b/solution.py
@@ -120,7 +120,7 @@
     )
     gain_local = jnp.sum(normed_grad * token_float * recip, axis=(0, 1, 2))
     loss_local = jnp.sum(sample_loss)
-    gain_total, loss_total = lax.psum((gain_local, loss_local), ("fsdp", "frame"))
+    gain_total, loss_total = lax.psum(lax.psum((gain_local, loss_local), "frame"), "fsdp")
     frame_count = frames_here * frame_devices
     gain_grad = gain_total / clip_count
     loss = loss_total / (clip_count * frame_count * patches * channels)

time: 435 us -> 459 us (1.055)
  blocking collectives: 40.4 us -> 67.6 us
    psum x1 -> x2, blocking collectives: 40.4 us -> 67.6 us  [the longest x1 57.9 us: per_device(): lax.psum(lax.psum((gain_local, loss_local), 'frame'), 'fsdp')]
  transfers between devices with their start and end apart: 7 -> 7, of which waited for: 3 -> 3; matrix products, arithmetic and copies ran while one was open for 21% -> 19% of each run, Pallas kernels for 0% -> 0%
where the time goes in v1:
time: 459 us; the launch traced here: 458 us
  waiting for transfers between devices  246 us (54%)
  blocking collectives  67.6 us (15%)
  matrix products  55.4 us (12%)
  other arithmetic  43 us (9%)
  local copies, waits for them, and re-layouts  23.3 us (5%)
  between operations  18.4 us (4%)
  starting transfers between devices  4.93 us (1%)
    unnamed x6, waiting for transfers between devices  172 us
    all_gather x1, waiting for transfers between devices, per_device(): weight = lax.all_gather(mae_weight, 'fsdp', axis=0, tiled=True)  65.8 us
    psum x1, blocking collectives, per_device(): lax.psum(lax.psum((gain_local, loss_local), 'frame'), 'fsdp')  57.9 us
    dot_general x2, matrix products, over_rows(): lax.dot_general(left, right, (((0,), (0,)), ((), ())), preferred_element_...  22.8 us
    convert_element_type x1, other arithmetic, per_device(): (recip * (norm_gain * normed_grad - token_float * recip * recip * inner))...  11.6 us
    dot_general x1, matrix products, back_project(): lax.dot_general(grads, weight, (((1,), (1,)), ((), ())), preferred_elemen...  10.6 us
    convert_element_type x1, local copies, waits for them, and re-layouts, per_device(): spread.reshape(samples, frames_here, patches, model_width)  10.4 us
    psum x1, blocking collectives, per_device(): lax.psum((gain_local, loss_local), 'frame')  9.72 us
  transfers between devices with their start and end apart: 7, of which 3 were waited for; matrix products, arithmetic and copies ran while one was open for 19% of the time, Pallas kernels for 0%

profile of v1, /device:TPU:0, one launch (start us, length us, event | category | flops | bytes accessed | tf_op | source)
XLA Modules:
  0.0 458.4 jit_solution(3298181236001652921)
XLA Ops:
  8.0 4.4 fusion.7
  12.7 2.6 fusion.2
  15.3 3.2 dynamic-slice_bitcast_fusion
  18.6 1.7 copy-done.1
  20.2 3.2 collective-permute-start.1
  25.3 65.8 %all-gather.4.cloned.1.call-done = bf16[3200,1408]{1,0:T(8,128)(2,1)} async-done(((bf16[200,1408]{1,0:T(8,128)(2,1)}), bf16[3200,1408]{1,0:T(8,128)(2,1)}) %all-gather.4.cloned.1.call-update) | async-done | bytes 9011216 | tf_op jit(solution)/shard_map/all_gather | solution.py:52
  91.1 9.5 %fusion.26 = f32[512,1408]{1,0:T(8,128)S(1)} fusion(bf16[512,3200]{1,0:T(8,128)(2,1)} %bitcast.116, bf16[3200,1408]{1,0:T(8,128)(2,1)} %all-gather.4.cloned.1.call-done), kind=kOutput, calls=%fused_computation.71 | convolution fusion | flops 4613734400 | bytes 15171584 | tf_op jit(solution)/shard_map/dot_general | solution.py:85
  100.7 7.5 %multiply_reduce_fusion.3 = (f32[512]{0:T(512)S(1)}, f32[512,1408]{1,0:T(8,128)S(1)}) fusion(f32[512,1408]{1,0:T(8,128)S(1)} %fusion.26, bf16[512,3200]{1,0:T(8,128)(2,1)} %bitcast.8, bf16[3200,1408]{1,0:T(8,128)(2,1)S(1)} %copy-done.7), kind=kOutput, calls=%fused_computation.31 | convolution fusion | flops 4616617472 | bytes 18057216 | tf_op jit(solution)/shard_map/dot_general | solution.py:86
  110.8 9.1 %fusion.27 = f32[3200,1408]{1,0:T(8,128)} fusion(bf16[512,3200]{1,0:T(8,128)(2,1)S(1)} %bitcast.117, bf16[512,1408]{1,0:T(8,128)(2,1)S(1)} %multiply_convert_fusion), kind=kOutput, calls=%fused_computation.72 | convolution fusion | flops 4613734400 | bytes 22740992 | tf_op jit(solution)/shard_map/dot_general | solution.py:23
  119.9 13.7 %add_multiply_fusion = f32[3200,1408]{1,0:T(8,128)} fusion(f32[3200,1408]{1,0:T(8,128)} %fusion.27, bf16[512,3200]{1,0:T(8,128)(2,1)} %bitcast.8, bf16[512,1408]{1,0:T(8,128)(2,1)S(1)} %multiply_convert_fusion), kind=kOutput, calls=%fused_computation.4 | convolution fusion | flops 4622745600 | bytes 40763392 | tf_op jit(solution)/shard_map/dot_general | solution.py:23
  133.7 10.6 %fusion.14 = bf16[512,3200]{1,0:T(8,128)(2,1)} fusion(bf16[512,1408]{1,0:T(8,128)(2,1)S(1)} %multiply_convert_fusion, bf16[3200,1408]{1,0:T(8,128)(2,1)} %all-gather.4.cloned.1.call-done), kind=kOutput, calls=%fused_computation.22 | convolution fusion | flops 4617011200 | bytes 13729792 | tf_op jit(solution)/shard_map/dot_general | solution.py:31
  144.3 1.5 collective-permute-start.2
  145.9 5.0 %fusion.12 = f32[4,1,3200]{2,1,0:T(1,128)S(1)} fusion(bf16[1,4,256,3200]{3,2,1,0:T(8,128)(2,1)} %copy-done.1, bf16[4,256,1]{1,0,2:T(4,128)(2,1)S(1)} %get-tuple-element.17), kind=kOutput, calls=%fused_computation.20 | convolution fusion | flops 6553600 | bytes 6606848 | tf_op jit(solution)/shard_map/bfp,bfpd->bfd/dot_general | solution.py:58
  153.3 170.9 %reduce-scatter.9.cloned.1.call-done = f32[200,1408]{1,0:T(8,128)} async-done(((f32[3200,1408]{1,0:T(8,128)}), f32[200,1408]{1,0:T(8,128)}) %reduce-scatter.9.cloned.1.call-update) | async-done | bytes 1126416
  324.2 2.8 copy.19
  327.1 8.7 %fusion.11 = f32[1,4,2,128,3200]{4,3,1,2,0:T(8,128)} fusion(bf16[1,4,1,128,3200]{4,3,1,2,0:T(8,128)(2,1)S(1)} %bitcast.118, bf16[1,4,1,128,3200]{4,3,1,2,0:T(8,128)(2,1)} %bitcast.11, pred[]{:T(512)S(6)} %eq.3), kind=kLoop, calls=%fused_computation.19 | loop fusion | flops 13107200 | bytes 19660800 | tf_op jit(solution)/shard_map/convert_element_type | solution.py:114
  335.8 10.4 %copy.15 = f32[1,4,2,128,3200]{4,3,2,1,0:T(8,128)} copy(f32[1,4,2,128,3200]{4,3,1,2,0:T(8,128)} %fusion.11) | data formatting | bytes 26214400 | tf_op jit(solution)/shard_map/convert_element_type | solution.py:114
  346.2 9.5 %fusion.10 = (f32[3200]{0:T(1024)S(1)}, f32[4,256]{1,0:T(4,128)S(1)}) fusion(bf16[1,4,256,3200]{3,2,1,0:T(8,128)(2,1)} %param.8, f32[1,4,2,128,3200]{4,3,2,1,0:T(8,128)} %copy.15, f32[4,3200]{1,0:T(4,128)S(1)} %fusion.20, f32[4,256]{1,0:T(4,128)S(1)} %get-tuple-element.16, f32[4,256]{1,0:T(4,128)S(1)} %add_rsqrt_fusion, f32[3200]{0:T(1024)S(1)} %copy-done.5), kind=kLoop, calls=%fused_computation.15 | loop fusion | flops 32763776 | bytes 19749888 | tf_op jit(solution)/shard_map/reduce_sum | solution.py:121
  355.7 9.7 %all-reduce.2 = (f32[3200]{0:T(1024)S(1)}, f32[]{:T(128)}) all-reduce(f32[3200]{0:T(1024)S(1)} %get-tuple-element.4, f32[]{:T(128)} %bitcast.30), channel_id=1, replica_groups=mesh['fsdp'=16,'frame'=2] {'frame'}, use_global_device_ids=true, to_apply=%region_11.12 | all-reduce | flops 3201 | bytes 25608 | tf_op jit(solution)/shard_map/psum | solution.py:123
  365.4 57.9 %all-reduce.1 = (f32[3200]{0:T(1024)S(1)}, f32[]{:T(128)}) all-reduce(f32[3200]{0:T(1024)S(1)} %get-tuple-element.12, f32[]{:T(128)} %get-tuple-element.13), channel_id=1, replica_groups=mesh['fsdp'=16,'frame'=2] {'fsdp'}, use_global_device_ids=true, to_apply=%region_12.13 | all-reduce | flops 3201 | bytes 25608 | tf_op jit(solution)/shard_map/psum | solution.py:123
  424.6 2.2 copy.20
  426.8 11.6 %fusion.6 = bf16[1,4,256,3200]{3,2,1,0:T(8,128)(2,1)} fusion(bf16[1,4,256,3200]{3,2,1,0:T(8,128)(2,1)} %param.8, f32[1,4,2,128,3200]{4,3,2,1,0:T(8,128)} %copy.15, f32[4,256]{1,0:T(4,128)S(1)} %broadcast_multiply_fusion.2, f32[4,3200]{1,0:T(4,128)S(1)} %fusion.20, f32[4,256]{1,0:T(4,128)S(1)} %get-tuple-element.16, f32[3200]{0:T(1024)S(1)} %copy-done.5, ...), kind=kLoop, calls=%fused_computation.11 | loop fusion | flops 36044800 | bytes 26290688 | tf_op jit(solution)/shard_map/convert_element_type | solution.py:118
  438.4 8.3 %all-gather.6.cloned.1.call-done = f32[2,704,200]{1,2,0:T(8,128)} async-done(((f32[1,704,200]{1,2,0:T(8,128)}), f32[2,704,200]{1,2,0:T(8,128)}) %all-gather.6.cloned.1.call-update) | async-done | bytes 1126416 | tf_op jit(solution)/shard_map/all_gather | solution.py:106
  448.7 2.0 reshape.268
  (50 shorter events, 8.2 us)
Async XLA Ops:
  7.2 5.2 %copy-start.5 = (f32[3200]{0:T(1024)S(1)}, f32[3200]{0:T(1024)}, u32[]{:S(2)}) copy-start(f32[3200]{0:T(1024)} %param.9) | copy-start | bytes 38404
  7.2 83.9 %all-gather.4.cloned.1.call-start = ((), (), s32[]{:S(2)}) async-start(), calls=%async_computation.2 | async-start | bytes 9574400 | tf_op jit(solution)/shard_map/all_gather | solution.py:52
  7.9 316.3 %reduce-scatter.9.cloned.1.call-start = ((), (), s32[]{:S(2)}) async-start(), calls=%async_computation.5 | async-start | bytes 19148800
  8.0 4.7 %copy-start = (bf16[1,4,256,3200]{3,2,1,0:T(8,128)(2,1)S(1)}, bf16[1,4,256,3200]{3,2,1,0:T(8,128)(2,1)}, u32[]{:S(2)}) copy-start(bf16[1,4,256,3200]{3,2,1,0:T(8,128)(2,1)} %param.8) | copy-start | bytes 19660804
  15.3 4.9 %copy-start.1 = (bf16[1,4,256,3200]{3,2,1,0:T(8,128)(2,1)}, bf16[1,4,256,3200]{3,2,1,0:T(8,128)(2,1)S(1)}, u32[]{:S(2)}) copy-start(bf16[1,4,256,3200]{3,2,1,0:T(8,128)(2,1)S(1)} %fusion.2) | copy-start | bytes 19660804
  15.3 8.2 %copy-start.6 = (s32[1,4,256]{2,1,0:T(4,128)S(1)}, s32[1,4,256]{2,1,0:T(4,128)}, u32[]{:S(2)}) copy-start(s32[1,4,256]{2,1,0:T(4,128)} %param.13) | copy-start | bytes 12292
  15.3 9.6 %copy-start.2 = (bf16[1,4,128,1408]{3,2,1,0:T(8,128)(2,1)S(1)}, bf16[1,4,128,1408]{3,2,1,0:T(8,128)(2,1)}, u32[]{:S(2)}) copy-start(bf16[1,4,128,1408]{3,2,1,0:T(8,128)(2,1)} %param.12) | copy-start | bytes 4325380
  20.2 80.4 %collective-permute-start.1 = (bf16[1,4,128,3200]{3,2,1,0:T(8,128)(2,1)}, bf16[1,4,128,3200]{3,2,1,0:T(8,128)(2,1)}, u32[]{:S(2)}, u32[]{:S(2)}) collective-permute-start(bf16[1,4,128,3200]{3,2,1,0:T(8,128)(2,1)} %get-tuple-element.14), channel_id=1, source_target_pairs={{0,1},{1,0},{2,3},{3,2},{4,5},{5,4},{6,7},{7,6},{8,9},{9,8},{10,11... | collective-permute-start | bytes 9830408 | tf_op jit(solution)/shard_map/ppermute | solution.py:10
  23.5 85.8 %collective-permute-start = (bf16[1,4,128]{2,1,0:T(4,128)(2,1)S(1)}, bf16[1,4,128]{2,1,0:T(4,128)(2,1)S(1)}, u32[]{:S(2)}, u32[]{:S(2)}) collective-permute-start(bf16[1,4,128]{2,1,0:T(4,128)(2,1)S(1)} %dynamic-slice_bitcast_fusion.1), channel_id=1, source_target_pairs={{0,1},{1,0},{2,3},{3,2},{4,5},{5,4},{6,7},{7,6},{8,9},{9,8},{10,11... | collective-permute-start | bytes 3080 | tf_op jit(solution)/shard_map/ppermute | solution.py:10
  91.1 9.6 %copy-start.7 = (bf16[3200,1408]{1,0:T(8,128)(2,1)S(1)}, bf16[3200,1408]{1,0:T(8,128)(2,1)}, u32[]{:S(2)}) copy-start(bf16[3200,1408]{1,0:T(8,128)(2,1)} %all-gather.4.cloned.1.call-done) | copy-start | bytes 27033604
  108.2 2.6 copy-start.3
  133.6 12.1 %copy-start.4 = (bf16[1,4,3200]{2,1,0:T(4,128)(2,1)S(1)}, bf16[1,4,3200]{2,1,0:T(4,128)(2,1)}, u32[]{:S(2)}) copy-start(bf16[1,4,3200]{2,1,0:T(4,128)(2,1)} %param.11) | copy-start | bytes 76804
  133.7 290.9 %reduce-scatter.7.cloned.1.call-start = ((), (), s32[]{:S(2)}) async-start(), calls=%async_computation.4 | async-start | bytes 2162688
  144.3 182.8 %collective-permute-start.2 = (bf16[1,4,128,3200]{3,2,1,0:T(8,128)(2,1)}, bf16[1,4,128,3200]{3,2,1,0:T(8,128)(2,1)S(1)}, u32[]{:S(2)}, u32[]{:S(2)}) collective-permute-start(bf16[1,4,128,3200]{3,2,1,0:T(8,128)(2,1)} %bitcast.12), channel_id=1, source_target_pairs={{0,1},{1,0},{2,3},{3,2},{4,5},{5,4},{6,7},{7,6},{8,9},{9,8},{10,11... | collective-permute-start | bytes 9830408 | tf_op jit(solution)/shard_map/ppermute | solution.py:10
  327.0 119.6 %all-gather.6.cloned.1.call-start = ((), (), s32[]{:S(2)}) async-start(), calls=%async_computation.3 | async-start | bytes 1843200 | tf_op jit(solution)/shard_map/all_gather | solution.py:106
Sparse Core Ops, SparseCore 0:
  10.1 80.9 all-gather.3
  133.8 190.4 reduce-scatter.8
  327.2 23.7 reduce-scatter.6
  426.9 19.7 all-gather.5
